TPU v7x, 32 devices: a whole 2x2x4 slice. The times are simulated.
32 devices in a mesh: grp: 2 (over x), dp: 8 (over z, y), tp: 2 (over core).
Axes of the slice: x: 2, y: 2, z: 4, core: 2. Of those that a mesh axis runs over, the one named last changes fastest.
Arguments:
- frames: bfloat16 [2, 16, 128, 1280], P('grp', ('dp', 'tp')), may hold values from -12 to 12
- counts: int32 [16], P('dp'), may hold values from 0 to 1, as said below
- w_qkv: bfloat16 [2, 1280, 3840], P('grp'), may hold values from -0.18727069 to 0.18727069
- ln_gain: bfloat16 [2, 1280], P('grp'), may hold values from 0.5 to 1.5
- w_proj: bfloat16 [2, 5120, 8192], P('grp', 'dp', 'tp'), may hold values from -1.5931984 to 1.5931984
- rms_gain: bfloat16 [2, 8192], P('grp', 'tp'), may hold values from 0.5 to 1.5
- cotangent: bfloat16 [2, 512, 8192], P('grp', 'dp', 'tp'), may hold values from -6 to 6
Outputs:
- frame_grad: bfloat16 [2, 16, 128, 1280], P('grp', ('dp', 'tp'))
Inputs may be any that keep to these rules, and one draw needn't show every extreme that they name: `counts`: some encoder device has all 1 frames live.
All inputs are finite; a program needn't handle non-finite values.
Results may differ from a plain program's by a relative error of at most 0.025.
Values may be sent and summed in bfloat16 or wider, within the bound.
No kernel may reach another device: no remote copies, remote signals or barrier semaphores. Data moves between devices by JAX's collectives and lax.ppermute only.
A program may use at most 128 MiB of HBM per device.

v0:
```python
import jax
import jax.numpy as jnp
from jax import lax
from jax.sharding import PartitionSpec as P

HEADS = 16
HDIM = 80
D = 8192


def passed_along(block, axis, distance):
    devices = range(lax.axis_size(axis))
    route = [(i - distance, i) for i in devices if i - distance in devices]
    return lax.ppermute(block, axis, route)


def encoder_forward(frames, w_qkv, ln_gain):
    frame_count = frames.shape[0]
    length = frames.shape[1]
    vis_width = frames.shape[2]
    mixed_qkv = jnp.einsum("fpe,ec->fpc", frames, w_qkv, preferred_element_type=jnp.float32).astype(
        jnp.bfloat16
    )
    split_heads = mixed_qkv.reshape(frame_count, length, 3, HEADS, HDIM)
    scores = jnp.einsum(
        "fqhd,fkhd->fhqk",
        split_heads[:, :, 0],
        split_heads[:, :, 1],
        preferred_element_type=jnp.float32,
    ) * HDIM ** (-0.5)
    attn_probs = jax.nn.softmax(scores, axis=-1)
    weights = attn_probs.astype(jnp.bfloat16)
    attended = jnp.einsum(
        "fhqk,fkhd->fqhd", weights, split_heads[:, :, 2], preferred_element_type=jnp.float32
    )
    summed = frames.astype(jnp.float32) + attended.reshape(frame_count, length, vis_width)
    centred = summed - jnp.mean(summed, axis=-1, keepdims=True)
    inverse = lax.rsqrt(jnp.mean(centred * centred, axis=-1, keepdims=True) + 1e-06)
    normal_part = centred * inverse
    embedded = (normal_part * ln_gain.astype(jnp.float32)).astype(jnp.bfloat16)
    return (
        embedded.reshape(frame_count * length // 4, 4 * vis_width),
        mixed_qkv,
        attn_probs,
        normal_part,
        inverse,
    )


def encoder_backward(w_qkv, ln_gain, mixed_qkv, attn_probs, normal_part, inverse, grad_embed):
    frame_count = normal_part.shape[0]
    length = normal_part.shape[1]
    vis_width = normal_part.shape[2]
    split_heads = mixed_qkv.reshape(frame_count, length, 3, HEADS, HDIM)
    query_heads = split_heads[:, :, 0]
    key_heads = split_heads[:, :, 1]
    value_heads = split_heads[:, :, 2]
    weights = attn_probs.astype(jnp.bfloat16)
    grad_norm = grad_embed.reshape(frame_count, length, vis_width).astype(
        jnp.float32
    ) * ln_gain.astype(jnp.float32)
    grad_summed = inverse * (
        grad_norm
        - jnp.mean(grad_norm, axis=-1, keepdims=True)
        - normal_part * jnp.mean(grad_norm * normal_part, axis=-1, keepdims=True)
    )
    grad_heads = grad_summed.astype(jnp.bfloat16).reshape(frame_count, length, HEADS, HDIM)
    grad_weights = jnp.einsum(
        "fqhd,fkhd->fhqk", grad_heads, value_heads, preferred_element_type=jnp.float32
    )
    grad_values = jnp.einsum(
        "fhqk,fqhd->fkhd", weights, grad_heads, preferred_element_type=jnp.float32
    ).astype(jnp.bfloat16)
    grad_scores = (
        attn_probs
        * (grad_weights - jnp.sum(grad_weights * attn_probs, axis=-1, keepdims=True))
        * HDIM ** (-0.5)
    ).astype(jnp.bfloat16)
    grad_query = jnp.einsum(
        "fhqk,fkhd->fqhd", grad_scores, key_heads, preferred_element_type=jnp.float32
    ).astype(jnp.bfloat16)
    grad_keys = jnp.einsum(
        "fhqk,fqhd->fkhd", grad_scores, query_heads, preferred_element_type=jnp.float32
    ).astype(jnp.bfloat16)
    grad_mixed = jnp.stack([grad_query, grad_keys, grad_values], axis=2).reshape(
        frame_count, length, 3 * vis_width
    )
    through = jnp.einsum("fpc,ec->fpe", grad_mixed, w_qkv, preferred_element_type=jnp.float32)
    return (grad_summed + through).astype(jnp.bfloat16)


def per_device(frames, counts, w_qkv, ln_gain, w_proj, rms_gain, cotangent):
    is_encoder = lax.axis_index("grp") == 0
    local_frames = frames[0]
    weight_mix = w_qkv[0]
    gain_ln = ln_gain[0]
    frame_count = local_frames.shape[0]
    length = local_frames.shape[1]
    vis_width = local_frames.shape[2]
    merged_width = 4 * vis_width
    tokens_frame = length // 4
    tokens_here = frame_count * tokens_frame

    def run_encoder():
        return encoder_forward(local_frames, weight_mix, gain_ln)

    def skip_encoder():
        return (
            jnp.zeros((tokens_here, merged_width), jnp.bfloat16),
            jnp.zeros((frame_count, length, 3 * vis_width), jnp.bfloat16),
            jnp.zeros((frame_count, HEADS, length, length), jnp.float32),
            jnp.zeros((frame_count, length, vis_width), jnp.float32),
            jnp.zeros((frame_count, length, 1), jnp.float32),
        )

    embedded, mixed_qkv, attn_probs, normal_part, inverse = lax.cond(
        is_encoder, run_encoder, skip_encoder
    )
    arrived = passed_along(embedded, "grp", 1)
    pooled = lax.all_gather(arrived, "tp", axis=0, tiled=True)
    full_proj = lax.all_gather(w_proj[0], "dp", axis=0, tiled=True)
    row_count = pooled.shape[0]
    col_count = full_proj.shape[1]
    activations = lax.cond(
        is_encoder,
        lambda: jnp.zeros((row_count, col_count), jnp.float32),
        lambda: jnp.dot(pooled, full_proj, preferred_element_type=jnp.float32),
    )
    tp_count = lax.axis_size("tp")
    position = lax.broadcasted_iota(jnp.int32, (row_count,), 0)
    source = position // tokens_here
    slot_index = position // tokens_frame % frame_count
    owner_hits = source[:, None] == lax.broadcasted_iota(jnp.int32, (1, tp_count), 1)
    live_limit = jnp.sum(jnp.where(owner_hits, counts[None, :], 0), axis=1)
    live_mask = (slot_index < live_limit).astype(jnp.float32)
    scaled = (
        rms_gain[0].astype(jnp.float32)[None, :]
        * cotangent[0].astype(jnp.float32)
        * live_mask[:, None]
    )
    squares = jnp.sum(activations * activations, axis=1)
    products = jnp.sum(activations * scaled, axis=1)
    total_sq, total_prod = lax.psum((squares, products), "tp")
    inverse_rms = lax.rsqrt(total_sq / D + 1e-06)[:, None]
    product = (total_prod / D)[:, None]
    grad_acts = (inverse_rms * scaled - activations * inverse_rms**3 * product).astype(jnp.bfloat16)
    term_rows = lax.cond(
        is_encoder,
        lambda: jnp.zeros((row_count, merged_width), jnp.bfloat16),
        lambda: lax.dot_general(
            grad_acts, full_proj, (((1,), (1,)), ((), ())), preferred_element_type=jnp.float32
        ).astype(jnp.bfloat16),
    )
    rounded_terms = lax.optimization_barrier(term_rows)
    summed_rows = lax.psum_scatter(
        rounded_terms.astype(jnp.float32).astype(jnp.bfloat16),
        "tp",
        scatter_dimension=0,
        tiled=True,
    )
    returned = passed_along(summed_rows, "grp", -1)
    grad_frames = lax.cond(
        is_encoder,
        lambda: encoder_backward(
            weight_mix, gain_ln, mixed_qkv, attn_probs, normal_part, inverse, returned
        ),
        lambda: jnp.zeros(local_frames.shape, jnp.bfloat16),
    )
    return grad_frames[None]


def solution(mesh):
    placed = (
        P("grp", ("dp", "tp"), None, None),
        P("dp"),
        P("grp", None, None),
        P("grp", None),
        P("grp", "dp", "tp"),
        P("grp", "tp"),
        P("grp", "dp", "tp"),
    )
    return jax.shard_map(
        per_device,
        mesh=mesh,
        in_specs=placed,
        out_specs=P("grp", ("dp", "tp"), None, None),
        check_vma=False,
    )
```

profile of v0, /device:TPU:0, one launch (start us, length us, event | category | flops | bytes accessed | tf_op | source)
XLA Modules:
  0.0 887.2 jit_solution(567608343134886291)
XLA Ops:
  6.5 0.0 all-gather.3.cloned.1.call-start
  6.5 0.7 all-gather.3.cloned.1.call-update
  7.3 0.0 reduce-scatter.2.cloned.1.call-start
  7.3 0.7 reduce.10
  8.0 0.0 copy-start.3
  8.0 0.0 copy-start.4
  8.0 19.9 %conditional.4 = (bf16[32,5120]{1,0:T(8,128)(2,1)}, bf16[1,128,3840]{2,1,0:T(8,128)(2,1)}, f32[1,16,128,128]{2,3,1,0:T(8,128)S(1)}, f32[1,128,1280]{2,1,0:T(8,128)S(1)}, f32[1,128,1]{1,2,0:T(1,128)S(1)}) conditional(s32[]{:T(128)} %convert_element_type.147, () %tuple.34, (bf16[1,1,128,1280]{3,2,1,0:T(8,128)(2,1)}, bf16[1280,3840]{1,0:T(8,128)(2,1)}, ...), branch_computations={%region_0.0_spmd, %region_1.0_spmd} | conditional | flops 1389332864 | bytes 39174724 | solution.py:116
  8.1 0.0 copy-start.1
  8.1 6.4 convolution_convert_fusion
  14.5 1.6 copy.33
  16.1 1.5 fusion.32
  17.6 1.4 convolution_multiply_fusion
  18.9 0.0 copy-done.1
  18.9 0.2 copy.36
  19.1 2.2 add_reduce_fusion
  21.3 0.2 copy.37
  21.5 0.2 multiply_reduce_fusion
  21.8 0.1 broadcast_multiply_fusion
  21.9 0.1 mul.117
  22.0 0.2 mul.118
  22.2 0.1 sub.62
  22.3 1.0 sub.63
  23.4 0.5 copy.35
  23.9 0.6 reshape.363
  24.5 0.2 reshape.373
  24.7 1.9 multiply_convert_fusion
  26.6 1.3 fusion.6
  28.0 1.3 collective-permute-start
  29.3 0.0 copy-done.3
  29.3 0.0 copy-done.4
  29.3 0.1 fusion.31
  29.4 8.0 collective-permute-done
  37.4 2.3 all_gather.6
  39.7 767.0 %all-gather.3.cloned.1.call-done = bf16[1,5120,4096]{2,1,0:T(8,128)(2,1)} async-done(((bf16[1,640,4096]{2,1,0:T(8,128)(2,1)}), bf16[1,5120,4096]{2,1,0:T(8,128)(2,1)}) %all-gather.3.cloned.1.call-update) | async-done | bytes 41943056 | tf_op jit(solution)/shard_map/all_gather | solution.py:121
  806.7 0.1 conditional.5
  806.7 0.1 broadcast.265
  806.7 1.4 multiply_reduce_fusion.3
  808.1 2.5 all-reduce
  810.6 1.4 fusion.29
  812.0 0.2 conditional.6
  812.2 0.0 copy-start.2
  812.2 0.8 copy-done.2
  813.0 0.0 reduce-scatter.2.cloned.1.call-update
  813.1 43.7 %reduce-scatter.2.cloned.1.call-done = bf16[32,5120]{1,0:T(8,128)(2,1)} async-done(((bf16[64,5120]{1,0:T(8,128)(2,1)}), bf16[32,5120]{1,0:T(8,128)(2,1)}) %reduce-scatter.2.cloned.1.call-update) | async-done | bytes 327696 | tf_op jit(solution)/shard_map/reduce_scatter | solution.py:155
  856.8 1.3 collective-permute-start.1
  858.1 10.6 %collective-permute-done.1 = bf16[32,5120]{1,0:T(8,128)(2,1)S(1)} collective-permute-done((bf16[32,5120]{1,0:T(8,128)(2,1)}, bf16[32,5120]{1,0:T(8,128)(2,1)S(1)}, u32[]{:S(2)}, u32[]{:S(2)}) %collective-permute-start.1) | collective-permute-done | bytes 327712 | tf_op jit(solution)/shard_map/ppermute | solution.py:14
  868.6 11.7 %conditional.7 = (bf16[1,1,128,1280]{3,2,1,0:T(8,128)(2,1)}) conditional(s32[]{:T(128)} %convert_element_type.147, () %tuple.33, (f32[1,128,1]{1,2,0:T(1,128)S(1)}, bf16[32,5120]{1,0:T(8,128)(2,1)S(1)}, bf16[1280]{0:T(1024)(128)(2,1)S(1)}, f32[1,128,1280]{2,1,0:T(8,128)S(1)}, bf16[1,128,3840]{2,1,0:T(8,128)(2,1)}, ...), branch_computations={%region_16.17_spmd, %region_17.21_spmd} | conditional | flops 1432157440 | bytes 69775912 | solution.py:162
  868.6 0.2 reshape.376
  868.8 0.2 multiply_reduce_fusion.2
  869.0 0.2 fusion.24
  869.2 0.9 copy.38
  870.1 1.6 copy.42
  871.7 0.0 copy-start
  871.7 1.5 fusion.19
  873.2 0.2 fusion.20
  873.4 0.3 fusion.16
  873.8 0.5 fusion.14
  874.3 1.8 fusion.15
  876.1 0.1 pad_maximum_fusion
  876.2 0.0 copy-done
  876.2 4.1 fusion.13
  (11 shorter events, 0.1 us)
Async XLA Ops:
  6.5 800.1 %all-gather.3.cloned.1.call-start = ((), (), s32[]{:S(2)}) async-start(), calls=%async_computation.2 | async-start | bytes 47185920 | tf_op jit(solution)/shard_map/all_gather | solution.py:121
  7.3 849.5 %reduce-scatter.2.cloned.1.call-start = ((), (), s32[]{:S(2)}) async-start(), calls=%async_computation.1 | async-start | bytes 983040 | tf_op jit(solution)/shard_map/reduce_scatter | solution.py:155
  8.0 21.2 %copy-start.3 = (bf16[1,4096]{1,0:T(2,128)(2,1)S(1)}, bf16[1,4096]{1,0:T(2,128)(2,1)}, u32[]{:S(2)}) copy-start(bf16[1,4096]{1,0:T(2,128)(2,1)} %param.20) | copy-start | bytes 24580
  8.0 21.3 %copy-start.4 = (s32[2]{0:T(128)S(1)}, s32[2]{0:T(128)}, u32[]{:S(2)}) copy-start(s32[2]{0:T(128)} %param.16) | copy-start | bytes 28
  8.1 10.9 %copy-start.1 = (bf16[1,1,128,1280]{3,2,1,0:T(8,128)(2,1)S(1)}, bf16[1,1,128,1280]{3,2,1,0:T(8,128)(2,1)}, u32[]{:S(2)}) copy-start(bf16[1,1,128,1280]{3,2,1,0:T(8,128)(2,1)} %get-tuple-element.69) | copy-start | bytes 983044 | tf_op jit(solution)/shard_map/cond
  28.0 9.5 %collective-permute-start = (bf16[32,5120]{1,0:T(8,128)(2,1)}, bf16[32,5120]{1,0:T(8,128)(2,1)S(1)}, u32[]{:S(2)}, u32[]{:S(2)}) collective-permute-start(bf16[32,5120]{1,0:T(8,128)(2,1)} %get-tuple-element.64), channel_id=1, source_target_pairs={{0,16},{1,17},{2,18},{3,19},{4,20},{5,21},{6,22},{7,23},{8,24},{9,... | collective-permute-start | bytes 983048 | tf_op jit(solution)/shard_map/ppermute | solution.py:14
  812.2 0.8 copy-start.2
  856.8 11.9 %collective-permute-start.1 = (bf16[32,5120]{1,0:T(8,128)(2,1)}, bf16[32,5120]{1,0:T(8,128)(2,1)S(1)}, u32[]{:S(2)}, u32[]{:S(2)}) collective-permute-start(bf16[32,5120]{1,0:T(8,128)(2,1)} %reduce-scatter.2.cloned.1.call-done), channel_id=1, source_target_pairs={{16,0},{17,1},{18,2},{19,3},{20,4},{21,5},{22,6},{23,7},{24,8},{25... | collective-permute-start | bytes 983048 | tf_op jit(solution)/shard_map/ppermute | solution.py:14
  871.7 4.5 copy-start
Sparse Core Ops, SparseCore 0:
  8.9 797.7 all-gather.2
  813.2 43.5 reduce-scatter.1
where the time goes:
time: 888 us; the launch traced here: 887 us
  waiting for transfers between devices  830 us (93%)
  matrix products  19.7 us (2%)
  between operations  13.5 us (2%)
    all_gather x1, waiting for transfers between devices, per_device(): full_proj = lax.all_gather(w_proj[0], 'dp', axis=0, tiled=True)  767 us
    reduce_scatter x1, waiting for transfers between devices, per_device(): lax.psum_scatter(rounded_terms.astype(jnp.float32).astype(jnp.bfloat16),...  43.7 us
    ppermute x2, waiting for transfers between devices, passed_along(): return lax.ppermute(block, axis, route)  18.6 us
  transfers between devices with their start and end apart: 4, of which 4 were waited for; matrix products, arithmetic and copies ran while one was open for 2% of the time, Pallas kernels for 0%

commit v1 on v0

--- a/solution.py
+++ b/solution.py
@@ -118,7 +118,14 @@
     )
     arrived = passed_along(embedded, "grp", 1)
     pooled = lax.all_gather(arrived, "tp", axis=0, tiled=True)
-    full_proj = lax.all_gather(w_proj[0], "dp", axis=0, tiled=True)
+    ways, here = (lax.axis_size("dp"), lax.axis_index("dp"))
+    full_proj, reach = (w_proj[0], 1)
+    while reach < ways:
+        theirs = lax.ppermute(full_proj, "dp", [(d, d ^ reach) for d in range(ways)])
+        mine_first = jnp.concatenate([full_proj, theirs], axis=0)
+        theirs_first = jnp.concatenate([theirs, full_proj], axis=0)
+        full_proj = jnp.where(here & reach == 0, mine_first, theirs_first)
+        reach = 2 * reach
     row_count = pooled.shape[0]
     col_count = full_proj.shape[1]
     activations = lax.cond(

time: 888 us -> 1420 us (1.60)
  waiting for transfers between devices: 830 us -> 1270 us
  other arithmetic: 7.89 us -> 87.9 us
    ppermute x0 -> x3, waiting for transfers between devices: none -> 1210 us  [per_device(): lax.ppermute(full_proj, 'dp', [(d, d ^ reach) for d in range(ways)])]
    all_gather x1 -> x0, waiting for transfers between devices: 767 us -> none  [per_device(): full_proj = lax.all_gather(w_proj[0], 'dp', axis=0, tiled=True)]
    select_n x0 -> x3, other arithmetic: none -> 80.5 us  [per_device(): full_proj = jnp.where(here & reach == 0, mine_first, theirs_first)]
  transfers between devices with their start and end apart: 4 -> 6, of which waited for: 4 -> 6; matrix products, arithmetic and copies ran while one was open for 2% -> 1% of each run, Pallas kernels for 0% -> 0%
where the time goes in v1:
time: 1420 us
  waiting for transfers between devices  1270 us (89%)
  other arithmetic  87.9 us (6%)
  matrix products  22.6 us (2%)
    ppermute x3, waiting for transfers between devices, per_device(): lax.ppermute(full_proj, 'dp', [(d, d ^ reach) for d in range(ways)])  1210 us
    select_n x3, other arithmetic, per_device(): full_proj = jnp.where(here & reach == 0, mine_first, theirs_first)  80.5 us
    reduce_scatter x1, waiting for transfers between devices, per_device(): lax.psum_scatter(rounded_terms.astype(jnp.float32).astype(jnp.bfloat16),...  44.5 us
  transfers between devices with their start and end apart: 6, of which 6 were waited for; matrix products, arithmetic and copies ran while one was open for 1% of the time, Pallas kernels for 0%

profile of v1, /device:TPU:0, one launch (start us, length us, event | category | flops | bytes accessed | tf_op | source)
XLA Modules:
  0.0 1415.8 jit_solution(12103879833148762540)
XLA Ops:
  6.5 0.0 reduce-scatter.2.cloned.1.call-start
  6.5 3.0 collective-permute-start.1
  9.5 113.4 %collective-permute-done.1 = bf16[640,4096]{1,0:T(8,128)(2,1)} collective-permute-done((bf16[640,4096]{1,0:T(8,128)(2,1)}, bf16[640,4096]{1,0:T(8,128)(2,1)}, u32[]{:S(2)}, u32[]{:S(2)}) %collective-permute-start.1) | collective-permute-done | bytes 5242912 | tf_op jit(solution)/shard_map/ppermute | solution.py:124
  122.9 13.7 maximum_select_fusion.2
  136.5 1.8 collective-permute-start.2
  138.3 225.1 %collective-permute-done.2 = bf16[1280,4096]{1,0:T(8,128)(2,1)} collective-permute-done((bf16[1280,4096]{1,0:T(8,128)(2,1)}, bf16[1280,4096]{1,0:T(8,128)(2,1)}, u32[]{:S(2)}, u32[]{:S(2)}) %collective-permute-start.2) | collective-permute-done | bytes 10485792 | tf_op jit(solution)/shard_map/ppermute | solution.py:124
  363.4 21.8 %maximum_select_fusion.1 = bf16[2560,4096]{1,0:T(8,128)(2,1)} fusion(bf16[1280,4096]{1,0:T(8,128)(2,1)} %collective-permute-done.2, bf16[1280,4096]{1,0:T(8,128)(2,1)} %maximum_select_fusion.2, pred[]{:T(512)S(6)} %eq.29), kind=kLoop, calls=%fused_computation.55 | loop fusion | flops 94371840 | bytes 41943040 | tf_op jit(solution)/shard_map/jit(_where)/select_n | solution.py:127
  385.2 2.6 collective-permute-start.3
  387.8 0.0 copy-done.3
  387.8 0.0 copy-done
  387.8 0.0 copy-start.2
  387.8 0.0 copy-start.4
  387.9 20.7 %conditional.4 = (bf16[32,5120]{1,0:T(8,128)(2,1)}, bf16[1,128,3840]{2,1,0:T(8,128)(2,1)}, f32[1,16,128,128]{2,3,1,0:T(8,128)S(1)}, f32[1,128,1280]{2,1,0:T(8,128)S(1)}, f32[1,128,1]{1,2,0:T(1,128)S(1)}) conditional(s32[]{:T(128)} %convert_element_type.147, () %tuple.34, (bf16[1,1,128,1280]{3,2,1,0:T(8,128)(2,1)S(1)}, bf16[1280,3840]{1,0:T(8,128)(2,1)}, ...), branch_computations={%region_0.0_spmd, %region_1.0_spmd} | conditional | flops 1389332864 | bytes 37863976 | solution.py:116
  387.9 6.2 convolution_convert_fusion
  394.1 1.6 copy.33
  395.7 1.5 fusion.32
  397.2 1.4 convolution_multiply_fusion
  398.6 0.2 copy.36
  398.7 2.1 add_reduce_fusion
  400.8 0.2 copy.37
  401.1 0.2 multiply_reduce_fusion
  401.3 0.1 broadcast_multiply_fusion
  401.4 0.1 mul.117
  401.6 1.0 mul.118
  402.6 0.1 sub.62
  402.7 1.0 sub.63
  403.7 0.5 copy.35
  404.2 0.6 reshape.363
  404.8 0.2 reshape.373
  405.1 2.1 multiply_convert_fusion
  407.2 1.3 fusion.6
  408.5 1.3 collective-permute-start
  409.8 0.0 copy-done.2
  409.9 0.0 copy-done.4
  409.9 0.1 fusion.31
  410.0 5.3 collective-permute-done
  415.3 2.3 all_gather.3
  417.6 868.7 %collective-permute-done.3 = bf16[2560,4096]{1,0:T(8,128)(2,1)} collective-permute-done((bf16[2560,4096]{1,0:T(8,128)(2,1)}, bf16[2560,4096]{1,0:T(8,128)(2,1)}, u32[]{:S(2)}, u32[]{:S(2)}) %collective-permute-start.3) | collective-permute-done | bytes 20971552 | tf_op jit(solution)/shard_map/ppermute | solution.py:124
  1286.3 45.1 %maximum_select_fusion = bf16[5120,4096]{1,0:T(8,128)(2,1)} fusion(bf16[2560,4096]{1,0:T(8,128)(2,1)} %collective-permute-done.3, bf16[2560,4096]{1,0:T(8,128)(2,1)} %maximum_select_fusion.1, pred[]{:T(512)S(6)} %eq.28), kind=kLoop, calls=%fused_computation.54 | loop fusion | flops 188743680 | bytes 83886080 | tf_op jit(solution)/shard_map/jit(_where)/select_n | solution.py:127
  1331.4 0.3 conditional.5
  1331.6 0.1 broadcast.265
  1331.6 1.4 multiply_reduce_fusion.3
  1333.0 2.5 all-reduce
  1335.5 1.4 fusion.29
  1336.9 0.1 conditional.6
  1336.9 0.0 copy-start.1
  1337.0 0.8 copy-done.1
  1337.8 0.0 reduce-scatter.2.cloned.1.call-update
  1337.8 44.5 %reduce-scatter.2.cloned.1.call-done = bf16[32,5120]{1,0:T(8,128)(2,1)} async-done(((bf16[64,5120]{1,0:T(8,128)(2,1)}), bf16[32,5120]{1,0:T(8,128)(2,1)}) %reduce-scatter.2.cloned.1.call-update) | async-done | bytes 327696 | tf_op jit(solution)/shard_map/reduce_scatter | solution.py:162
  1382.3 1.3 collective-permute-start.4
  1383.5 10.6 collective-permute-done.4
  1394.1 14.8 %conditional.7 = (bf16[1,1,128,1280]{3,2,1,0:T(8,128)(2,1)}) conditional(s32[]{:T(128)} %convert_element_type.147, () %tuple.33, (f32[1,128,1]{1,2,0:T(1,128)S(1)}, bf16[32,5120]{1,0:T(8,128)(2,1)S(1)}, bf16[1280]{0:T(1024)(128)(2,1)S(1)}, f32[1,128,1280]{2,1,0:T(8,128)S(1)}, bf16[1,128,3840]{2,1,0:T(8,128)(2,1)}, ...), branch_computations={%region_16.17_spmd, %region_17.21_spmd} | conditional | flops 1432157440 | bytes 30454280 | solution.py:169
  1394.1 0.2 reshape.376
  1394.3 0.2 multiply_reduce_fusion.2
  1394.5 0.2 fusion.24
  1394.7 0.9 copy.38
  1395.6 1.6 copy.42
  1397.2 1.3 fusion.19
  1398.5 0.2 fusion.20
  1398.8 0.3 fusion.16
  1399.1 0.5 fusion.14
  1399.6 1.5 fusion.15
  1401.0 0.1 pad_maximum_fusion
  1401.2 7.8 fusion.13
  (14 shorter events, 0.2 us)
Async XLA Ops:
  6.5 1375.7 %reduce-scatter.2.cloned.1.call-start = ((), (), s32[]{:S(2)}) async-start(), calls=%async_computation.1 | async-start | bytes 983040 | tf_op jit(solution)/shard_map/reduce_scatter | solution.py:162
  6.5 116.3 %collective-permute-start.1 = (bf16[640,4096]{1,0:T(8,128)(2,1)}, bf16[640,4096]{1,0:T(8,128)(2,1)}, u32[]{:S(2)}, u32[]{:S(2)}) collective-permute-start(bf16[640,4096]{1,0:T(8,128)(2,1)} %bitcast.136), channel_id=1, source_target_pairs={{0,2},{2,0},{4,6},{6,4},{8,10},{10,8},{12,14},{14,12},{1,3},{3,1},... | collective-permute-start | bytes 15728648 | tf_op jit(solution)/shard_map/ppermute | solution.py:124
  136.5 226.9 %collective-permute-start.2 = (bf16[1280,4096]{1,0:T(8,128)(2,1)}, bf16[1280,4096]{1,0:T(8,128)(2,1)}, u32[]{:S(2)}, u32[]{:S(2)}) collective-permute-start(bf16[1280,4096]{1,0:T(8,128)(2,1)} %maximum_select_fusion.2), channel_id=1, source_target_pairs={{0,4},{2,6},{4,0},{6,2},{8,12},{10,14},{12,8},{14,10},{1,5},{3,7},... | collective-permute-start | bytes 31457288 | tf_op jit(solution)/shard_map/ppermute | solution.py:124
  138.3 249.5 %copy-start.3 = (bf16[1,1280]{1,0:T(2,128)(2,1)S(1)}, bf16[1,1280]{1,0:T(2,128)(2,1)}, u32[]{:S(2)}) copy-start(bf16[1,1280]{1,0:T(2,128)(2,1)} %param.18) | copy-start | bytes 7684
  138.3 249.5 %copy-start = (bf16[1,1,128,1280]{3,2,1,0:T(8,128)(2,1)S(1)}, bf16[1,1,128,1280]{3,2,1,0:T(8,128)(2,1)}, u32[]{:S(2)}) copy-start(bf16[1,1,128,1280]{3,2,1,0:T(8,128)(2,1)} %param.15) | copy-start | bytes 983044
  385.2 901.1 %collective-permute-start.3 = (bf16[2560,4096]{1,0:T(8,128)(2,1)}, bf16[2560,4096]{1,0:T(8,128)(2,1)}, u32[]{:S(2)}, u32[]{:S(2)}) collective-permute-start(bf16[2560,4096]{1,0:T(8,128)(2,1)} %maximum_select_fusion.1), channel_id=1, source_target_pairs={{0,8},{2,10},{4,12},{6,14},{8,0},{10,2},{12,4},{14,6},{1,9},{3,11}... | collective-permute-start | bytes 62914568 | tf_op jit(solution)/shard_map/ppermute | solution.py:124
  387.8 22.0 %copy-start.2 = (bf16[1,4096]{1,0:T(2,128)(2,1)S(1)}, bf16[1,4096]{1,0:T(2,128)(2,1)}, u32[]{:S(2)}) copy-start(bf16[1,4096]{1,0:T(2,128)(2,1)} %param.20) | copy-start | bytes 24580
  387.8 22.1 %copy-start.4 = (s32[2]{0:T(128)S(1)}, s32[2]{0:T(128)}, u32[]{:S(2)}) copy-start(s32[2]{0:T(128)} %param.16) | copy-start | bytes 28
  408.5 6.8 collective-permute-start
  1336.9 0.8 copy-start.1
  1382.3 11.9 collective-permute-start.4
Sparse Core Ops, SparseCore 0:
  1337.9 44.2 reduce-scatter.1
